TPU v7x, 256 devices: a whole 4x4x8 slice. The times are simulated.
256 devices in a mesh: group: 8 (over x, core), member: 32 (over y, z).
Axes of the slice: x: 4, y: 4, z: 8, core: 2. Of those that a mesh axis runs over, the one named last changes fastest.
Arguments:
- q_rows: bfloat16 [65536, 8192], P(('group', 'member')), may hold values from -36 to 36
- own_kv: bfloat16 [65536, 1024], P(('group', 'member')), may hold values from -6 to 6
- cache: bfloat16 [1024, 64, 1024], P(('group', 'member')), may hold values from -6 to 6
- recomp_hidden: bfloat16 [512, 8, 16, 4096], P(('group', 'member')), may hold values from -6 to 6
- w_kv: bfloat16 [4096, 1024], P('member', 'group'), may hold values from -0.09375 to 0.09375
- retrieval: int32 [512, 8], P(('group', 'member')), may hold values from 0 to 127, as said below
- positions: int32 [512, 8, 16], P(('group', 'member')), may hold values from 0 to 63, as said below
Outputs:
- attn_out: bfloat16 [65536, 8192], P(('group', 'member'))
Inputs may be any that keep to these rules, and one draw needn't show every extreme that they name: `retrieval`: the 8 passages of one query are different. Passage i of a group's corpus is held by the device of member index i // 4 in that group. The queries of one device name at most 1 passages held by any one device, and this bound is reached. The 16 positions of one retrieved passage are different.
All inputs are finite; a program needn't handle non-finite values.
Results may differ from a plain program's by a relative error of at most 0.0054.
Values may be sent and summed in bfloat16 or wider, within the bound.
A program may use at most 128 MiB of HBM per device.

v0:
```python
import jax
import jax.numpy as jnp
from jax import lax
from jax.sharding import PartitionSpec as P

D = 4096
HQ = 64
KVH = 4
HD = 128
TOPP = 8
QLEN = 128
PLEN = 64
RECOMP = 16
EPSILON = 1e-06


def local(q_rows, own_kv, cache, recomp_hidden, w_kv, retrieval, positions):
    query_count = retrieval.shape[0]
    requests = query_count * TOPP
    kv_width = 2 * KVH * HD
    grouped = HQ // KVH
    span_keys = TOPP * PLEN + QLEN
    scale = 1.0 / HD**0.5
    row_count = requests * RECOMP
    hidden = recomp_hidden.reshape(row_count, D).astype(jnp.float32)
    normed = (
        hidden * lax.rsqrt(jnp.mean(hidden * hidden, axis=1, keepdims=True) + EPSILON)
    ).astype(jnp.bfloat16)
    head_columns = lax.all_gather(w_kv, "group", axis=1, tiled=True)
    projected = jnp.dot(
        normed,
        lax.all_gather(head_columns, "member", axis=0, tiled=True),
        preferred_element_type=jnp.float32,
    )
    recomputed = projected.astype(jnp.bfloat16).reshape(requests, RECOMP, kv_width)
    wanted = retrieval.reshape(requests)
    pass_local = cache.shape[0]
    holders_count = lax.axis_size("member")
    my_index = lax.axis_index("member")
    capacity = -(-requests // holders_count)
    request_table = lax.all_gather(wanted.reshape(1, requests), "member", axis=0, tiled=True)
    mine_mask = request_table // pass_local == my_index
    earlier_mask = (jnp.arange(requests)[:, None] < jnp.arange(requests)[None, :]).astype(jnp.int32)
    slot_rank = jnp.dot(mine_mask.astype(jnp.int32), earlier_mask)
    slot_table = mine_mask[:, None, :] & (
        slot_rank[:, None, :] == jnp.arange(capacity)[None, :, None]
    )
    local_index = jnp.sum(
        jnp.where(slot_table, (request_table % pass_local)[:, None, :], 0), axis=2
    )
    slot_filled = jnp.any(slot_table, axis=2)
    outgoing = jnp.where(
        slot_filled[:, :, None, None], cache[local_index], jnp.zeros((), cache.dtype)
    )
    arrived = lax.all_to_all(outgoing, "member", split_axis=0, concat_axis=0, tiled=True)
    holder_of = wanted // pass_local
    same_holder = holder_of[:, None] == holder_of[None, :]
    before_me = jnp.arange(requests)[None, :] < jnp.arange(requests)[:, None]
    copy_rank = jnp.sum((same_holder & before_me).astype(jnp.int32), axis=1)
    blocks = arrived.reshape(holders_count * capacity, PLEN, kv_width)[
        holder_of * capacity + copy_rank
    ]
    spots = positions.reshape(requests, RECOMP)
    onehot = spots[:, :, None] == jnp.arange(PLEN)[None, None, :]
    covered = jnp.any(onehot, axis=1)
    placed = jnp.einsum(
        "krp,kre->kpe", onehot.astype(jnp.bfloat16), recomputed, preferred_element_type=jnp.float32
    ).astype(jnp.bfloat16)
    context = jnp.where(covered[:, :, None], placed, blocks).reshape(
        query_count, TOPP * PLEN, kv_width
    )
    context = jnp.concatenate([context, own_kv.reshape(query_count, QLEN, kv_width)], axis=1)
    keys = context[:, :, : KVH * HD].reshape(query_count, span_keys, KVH, HD)
    values = context[:, :, KVH * HD :].reshape(query_count, span_keys, KVH, HD)
    queries = q_rows.reshape(query_count, QLEN, KVH, grouped, HD)
    token_pos = jnp.arange(QLEN)[:, None]
    key_pos = jnp.arange(span_keys)[None, :]
    visible = (key_pos < TOPP * PLEN) | (key_pos - TOPP * PLEN <= token_pos)

    def attend(operands):
        query_block, key_block, value_block = operands
        scores = (
            jnp.einsum("tkgd,skd->kgts", query_block, key_block, preferred_element_type=jnp.float32)
            * scale
        )
        scores = jnp.where(visible, scores, -jnp.inf)
        peak = jnp.max(scores, axis=-1, keepdims=True)
        expd = jnp.exp(scores - peak)
        probs = (expd / jnp.sum(expd, axis=-1, keepdims=True)).astype(jnp.bfloat16)
        output = jnp.einsum(
            "kgts,skd->tkgd", probs, value_block, preferred_element_type=jnp.float32
        )
        return output.astype(jnp.bfloat16).reshape(QLEN, HQ * HD)

    results = lax.map(attend, (queries, keys, values))
    return results.reshape(query_count * QLEN, HQ * HD)


def solution(mesh):
    placed = (
        P(("group", "member"), None),
        P(("group", "member"), None),
        P(("group", "member"), None, None),
        P(("group", "member"), None, None, None),
        P("member", "group"),
        P(("group", "member"), None),
        P(("group", "member"), None, None),
    )
    return jax.shard_map(
        local, mesh=mesh, in_specs=placed, out_specs=P(("group", "member"), None), check_vma=False
    )
```

profile of v0, /device:TPU:32, one launch (start us, length us, event | category | flops | bytes accessed | tf_op | source)
XLA Modules:
  0.0 287.2 jit_solution(2852515802772880683)
XLA Ops:
  6.5 13.6 %all_gather.9 = bf16[128,1024]{1,0:T(8,128)(2,1)} all-gather(bf16[128,128]{1,0:T(8,128)(2,1)} %param.13), channel_id=1, replica_groups=mesh['group'=8,'member'=32] {'group'}, dimensions={1}, use_global_device_ids=true | all-gather | bytes 294912 | tf_op jit(solution)/shard_map/all_gather | solution.py:29
  21.0 40.2 %all-gather = s32[32,1,16]{2,1,0:T(1,128)S(1)} all-gather(s32[1,1,16]{2,1,0:T(1,128)S(1)} %reshape.252), channel_id=1, replica_groups=mesh['group'=8,'member'=32] {'member'}, dimensions={0}, use_global_device_ids=true | all-gather | bytes 2112 | tf_op jit(solution)/shard_map/all_gather | solution.py:41
  61.5 2.8 gather_fusion
  64.4 4.5 %bitcast_select_fusion.4 = bf16[32,1,64,1024]{3,2,1,0:T(8,128)(2,1)} fusion(bf16[32,64,1024]{2,1,0:T(8,128)(2,1)} %gather_fusion, pred[32]{0:T(512)(128)(4,1)S(1)} %reduce_or.19), kind=kLoop, calls=%fused_computation.31 | loop fusion | flops 2097152 | bytes 8388640 | tf_op jit(solution)/shard_map/jit(_where)/select_n | solution.py:52
  68.9 8.1 %all-to-all-start = ((bf16[32,1,64,1024]{3,2,1,0:T(8,128)(2,1)}), bf16[32,1,64,1024]{3,2,1,0:T(8,128)(2,1)}, u32[]{:S(2)}, u32[]{:S(2)}) async-start(bf16[32,1,64,1024]{3,2,1,0:T(8,128)(2,1)} %bitcast_select_fusion.4), calls=%async_computation | async-start | bytes 8388608 | tf_op jit(solution)/shard_map/all_to_all | solution.py:55
  78.1 5.4 %copy.46 = bf16[32,8,64,128]{3,2,1,0:T(8,128)(2,1)} copy(bf16[32,8,64,128]{3,1,2,0:T(8,128)(2,1)} %bitcast.134) | data formatting | bytes 8388608
  83.8 1.9 fusion.30
  85.7 118.0 %all-to-all-done = bf16[32,1,64,1024]{3,2,1,0:T(8,128)(2,1)} async-done(((bf16[32,1,64,1024]{3,2,1,0:T(8,128)(2,1)}), bf16[32,1,64,1024]{3,2,1,0:T(8,128)(2,1)}, u32[]{:S(2)}, u32[]{:S(2)}) %all-to-all-start) | async-done | bytes 4194336 | tf_op jit(solution)/shard_map/all_to_all | solution.py:55
  203.7 2.9 gather_fusion.1
  206.6 6.3 %convolution_convert_fusion = bf16[256,1024]{1,0:T(8,128)(2,1)S(1)} fusion(bf16[256,4096]{1,0:T(8,128)(2,1)} %fusion.30, bf16[4096,1024]{1,0:T(8,128)(2,1)} %all-gather.3.cloned.1.call-done), kind=kOutput, calls=%fused_computation.40 | convolution fusion | flops 2147745792 | bytes 11010048 | tf_op jit(solution)/shard_map/dot_general | solution.py:30
  213.0 2.6 convert_select_fusion
  215.6 2.9 copy.34
  218.4 1.7 pad_maximum_fusion
  220.2 59.2 %while.11 = (s32[]{:T(128)}, bf16[2,128,8192]{2,1,0:T(8,128)(2,1)}, bf16[2,640,4,128]{1,3,2,0:T(8,128)(2,1)}, bf16[2,640,4,128]{1,3,2,0:T(8,128)(2,1)}, bf16[2,1...) while((s32[]{:T(128)}, bf16[2,128,8192]{2,1,0:T(8,128)(2,1)}, ...), condition=%wide.region_8.9_spmd.clone, body=%wide.region_5.8_spmd.clone.sunk | while | flops 2717024768 | bytes 60265176 | solution.py:95
  220.2 2.0 constant_dynamic-slice_fusion.2
  222.4 12.5 %fusion.73 = (f32[4,16,128]{2,1,0:T(8,128)S(1)}, f32[4,16,128,640]{2,3,1,0:T(8,128)}) fusion(pred[128,640]{0,1:T(8,128)(4,1)S(1)} %fusion.72, bf16[1,128,4,16,128]{4,3,2,1,0:T(8,128)(2,1)S(1)} %constant_dynamic-slice_fusion.2, bf16[2,640,4,128]{1,3,2,0:T(8,128)(2,1)} %get-tuple-element.170, s32[]{:T(128)} %get-tuple-element.159), kind=kOutput, calls=%fused_computation.92.clone.1 | convolution fusion | flops 1363149440 | bytes 23839232 | tf_op jit(solution)/shard_map/while/body/eval_jaxpr/sub | solution.py:88
  234.9 10.4 %fusion.74 = bf16[4,128,16,128]{3,1,2,0:T(8,128)(2,1)} fusion(f32[4,16,128,640]{2,3,1,0:T(8,128)} %get-tuple-element.149, f32[4,16,128]{2,1,0:T(8,128)S(1)} %get-tuple-element.150, bf16[2,640,4,128]{1,3,2,0:T(8,128)(2,1)} %get-tuple-element.169, s32[]{:T(128)} %get-tuple-element.159), kind=kOutput, calls=%fused_computation.14.clone.1 | convolution fusion | flops 1353711616 | bytes 23757312 | tf_op jit(solution)/shard_map/while/body/eval_jaxpr/kgts,skd->tkgd/dot_general | solution.py:90
  245.4 2.9 %copy.61 = bf16[1,128,8192]{2,1,0:T(8,128)(2,1)S(1)} copy(bf16[1,128,8192]{1,2,0:T(8,128)(2,1)} %bitcast.131) | data formatting | bytes 4194304 | tf_op jit(solution)/shard_map/while/body/jit(dynamic_update_index_in_dim)/dynamic_update_slice | solution.py:95
  248.3 1.5 constant_dynamic-update-slice_fusion.2
  249.8 2.0 constant_dynamic-slice_fusion.2
  252.0 12.5 %fusion.73 = (f32[4,16,128]{2,1,0:T(8,128)S(1)}, f32[4,16,128,640]{2,3,1,0:T(8,128)}) fusion(pred[128,640]{0,1:T(8,128)(4,1)S(1)} %fusion.72, bf16[1,128,4,16,128]{4,3,2,1,0:T(8,128)(2,1)S(1)} %constant_dynamic-slice_fusion.2, bf16[2,640,4,128]{1,3,2,0:T(8,128)(2,1)} %get-tuple-element.170, s32[]{:T(128)} %get-tuple-element.159), kind=kOutput, calls=%fused_computation.92.clone.1 | convolution fusion | flops 1363149440 | bytes 23839232 | tf_op jit(solution)/shard_map/while/body/eval_jaxpr/sub | solution.py:88
  264.5 10.4 %fusion.74 = bf16[4,128,16,128]{3,1,2,0:T(8,128)(2,1)} fusion(f32[4,16,128,640]{2,3,1,0:T(8,128)} %get-tuple-element.149, f32[4,16,128]{2,1,0:T(8,128)S(1)} %get-tuple-element.150, bf16[2,640,4,128]{1,3,2,0:T(8,128)(2,1)} %get-tuple-element.169, s32[]{:T(128)} %get-tuple-element.159), kind=kOutput, calls=%fused_computation.14.clone.1 | convolution fusion | flops 1353711616 | bytes 23757312 | tf_op jit(solution)/shard_map/while/body/eval_jaxpr/kgts,skd->tkgd/dot_general | solution.py:90
  275.0 2.9 %copy.61 = bf16[1,128,8192]{2,1,0:T(8,128)(2,1)S(1)} copy(bf16[1,128,8192]{1,2,0:T(8,128)(2,1)} %bitcast.131) | data formatting | bytes 4194304 | tf_op jit(solution)/shard_map/while/body/jit(dynamic_update_index_in_dim)/dynamic_update_slice | solution.py:95
  277.9 1.5 constant_dynamic-update-slice_fusion.2
  (37 shorter events, 4.0 us)
Async XLA Ops:
  6.5 55.0 %copy-start = (bf16[4,64,1024]{2,1,0:T(8,128)(2,1)S(1)}, bf16[4,64,1024]{2,1,0:T(8,128)(2,1)}, u32[]{:S(2)}) copy-start(bf16[4,64,1024]{2,1,0:T(8,128)(2,1)} %param.11) | copy-start | bytes 1572868
  6.5 200.1 %all-gather.3.cloned.1.call-start = ((), (), s32[]{:S(2)}) async-start(), calls=%async_computation.1 | async-start | bytes 8650752 | tf_op jit(solution)/shard_map/all_gather | solution.py:32
  68.9 8.1 %copy-start.5 = (s32[2,8]{1,0:T(2,128)S(1)}, s32[2,8]{1,0:T(2,128)}, u32[]{:S(2)}) copy-start(s32[2,8]{1,0:T(2,128)} %param.14) | copy-start | bytes 196
  68.9 8.3 %copy-start.2 = (bf16[2,8,16,4096]{3,2,1,0:T(8,128)(2,1)S(1)}, bf16[2,8,16,4096]{3,2,1,0:T(8,128)(2,1)}, u32[]{:S(2)}) copy-start(bf16[2,8,16,4096]{3,2,1,0:T(8,128)(2,1)} %param.12) | copy-start | bytes 6291460
  68.9 8.9 %copy-start.3 = (bf16[256,1024]{1,0:T(8,128)(2,1)S(1)}, bf16[256,1024]{1,0:T(8,128)(2,1)}, u32[]{:S(2)}) copy-start(bf16[256,1024]{1,0:T(8,128)(2,1)} %param.10) | copy-start | bytes 1572868
  68.9 134.8 %all-to-all-start = ((bf16[32,1,64,1024]{3,2,1,0:T(8,128)(2,1)}), bf16[32,1,64,1024]{3,2,1,0:T(8,128)(2,1)}, u32[]{:S(2)}, u32[]{:S(2)}) async-start(bf16[32,1,64,1024]{3,2,1,0:T(8,128)(2,1)} %bitcast_select_fusion.4), calls=%async_computation | async-start | bytes 8388608 | tf_op jit(solution)/shard_map/all_to_all | solution.py:55
  78.0 5.6 %copy-start.4 = (s32[2,8,16]{2,1,0:T(8,128)S(1)}, s32[2,8,16]{2,1,0:T(8,128)}, u32[]{:S(2)}) copy-start(s32[2,8,16]{2,1,0:T(8,128)} %param.15) | copy-start | bytes 3076
  279.4 1.0 copy-start.1
Sparse Core Ops, SparseCore 0:
  20.3 181.5 all-gather.2
where the time goes:
time: 288 us; the launch traced here: 287 us
  waiting for transfers between devices  118 us (41%)
  matrix products  55.1 us (19%)
  blocking collectives  53.9 us (19%)
  local copies, waits for them, and re-layouts  29.1 us (10%)
  between operations  13.5 us (5%)
  other arithmetic  9.49 us (3%)
  starting transfers between devices  8.12 us (3%)
    all_to_all x1, waiting for transfers between devices, local(): lax.all_to_all(outgoing, 'member', split_axis=0, concat_axis=0, tiled=True)  118 us
    all_gather x1, blocking collectives, local(): lax.all_gather(wanted.reshape(1, requests), 'member', axis=0, tiled=True)  40.2 us
    sub x2, matrix products, attend(): expd = jnp.exp(scores - peak)  25.1 us
    dot_general x2, matrix products, attend(): jnp.einsum('kgts,skd->tkgd', probs, value_block, preferred_element_type=j...  20.9 us
    all_gather x1, blocking collectives, local(): head_columns = lax.all_gather(w_kv, 'group', axis=1, tiled=True)  13.6 us
    dynamic_update_slice x4, local copies, waits for them, and re-layouts, local(): results = lax.map(attend, (queries, keys, values))  8.71 us
    all_to_all x1, starting transfers between devices, local(): lax.all_to_all(outgoing, 'member', split_axis=0, concat_axis=0, tiled=True)  8.12 us
    unnamed x14, local copies, waits for them, and re-layouts  7.19 us
  transfers between devices with their start and end apart: 2, of which 1 were waited for; matrix products, arithmetic and copies ran while one was open for 7% of the time, Pallas kernels for 0%

commit v1 on v0

--- a/solution.py
+++ b/solution.py
@@ -12,6 +12,11 @@
 PLEN = 64
 RECOMP = 16
 EPSILON = 1e-06
+
+
+def gather_from_all(value, axis, dim):
+    copies = jnp.concatenate([value] * lax.axis_size(axis), axis=dim)
+    return lax.all_to_all(copies, axis, dim, dim, tiled=True)
 
 
 def local(q_rows, own_kv, cache, recomp_hidden, w_kv, retrieval, positions):
@@ -38,7 +43,7 @@
     holders_count = lax.axis_size("member")
     my_index = lax.axis_index("member")
     capacity = -(-requests // holders_count)
-    request_table = lax.all_gather(wanted.reshape(1, requests), "member", axis=0, tiled=True)
+    request_table = gather_from_all(wanted.reshape(1, requests), "member", 0)
     mine_mask = request_table // pass_local == my_index
     earlier_mask = (jnp.arange(requests)[:, None] < jnp.arange(requests)[None, :]).astype(jnp.int32)
     slot_rank = jnp.dot(mine_mask.astype(jnp.int32), earlier_mask)

time: 288 us -> 272 us (0.944)
  blocking collectives: 53.9 us -> 13.6 us
  waiting for transfers between devices: 118 us -> 131 us
  starting transfers between devices: 8.12 us -> 17.5 us
    all_gather x1 -> x0, blocking collectives: 40.2 us -> none  [local(): lax.all_gather(wanted.reshape(1, requests), 'member', axis=0, tiled=True)]
    all_to_all x0 -> x1, starting transfers between devices: none -> 11.4 us  [gather_from_all(): return lax.all_to_all(copies, axis, dim, dim, tiled=True)]
    all_to_all x0 -> x1, waiting for transfers between devices: none -> 8.6 us  [gather_from_all(): return lax.all_to_all(copies, axis, dim, dim, tiled=True)]
    all_to_all x1, waiting for transfers between devices: 118 us -> 123 us  [local(): lax.all_to_all(outgoing, 'member', split_axis=0, concat_axis=0, tiled=True)]
    unnamed x14 -> x13, local copies, waits for them, and re-layouts: 7.19 us -> 6.43 us
  transfers between devices with their start and end apart: 2 -> 3, of which waited for: 1 -> 2; matrix products, arithmetic and copies ran while one was open for 7% -> 8% of each run, Pallas kernels for 0% -> 0%
where the time goes in v1:
time: 272 us; the launch traced here: 270 us
  waiting for transfers between devices  131 us (48%)
  matrix products  55.1 us (20%)
  local copies, waits for them, and re-layouts  29.6 us (11%)
  starting transfers between devices  17.5 us (6%)
  blocking collectives  13.6 us (5%)
  between operations  13.5 us (5%)
  other arithmetic  9.49 us (3%)
    all_to_all x1, waiting for transfers between devices, local(): lax.all_to_all(outgoing, 'member', split_axis=0, concat_axis=0, tiled=True)  123 us
    sub x2, matrix products, attend(): expd = jnp.exp(scores - peak)  25.1 us
    dot_general x2, matrix products, attend(): jnp.einsum('kgts,skd->tkgd', probs, value_block, preferred_element_type=j...  20.9 us
    all_gather x1, blocking collectives, local(): head_columns = lax.all_gather(w_kv, 'group', axis=1, tiled=True)  13.6 us
    all_to_all x1, starting transfers between devices, gather_from_all(): return lax.all_to_all(copies, axis, dim, dim, tiled=True)  11.4 us
    dynamic_update_slice x4, local copies, waits for them, and re-layouts, local(): results = lax.map(attend, (queries, keys, values))  8.71 us
    all_to_all x1, waiting for transfers between devices, gather_from_all(): return lax.all_to_all(copies, axis, dim, dim, tiled=True)  8.6 us
    unnamed x13, local copies, waits for them, and re-layouts  6.43 us
  transfers between devices with their start and end apart: 3, of which 2 were waited for; matrix products, arithmetic and copies ran while one was open for 8% of the time, Pallas kernels for 0%

profile of v1, /device:TPU:32, one launch (start us, length us, event | category | flops | bytes accessed | tf_op | source)
XLA Modules:
  0.0 270.3 jit_solution(10718499953830397325)
XLA Ops:
  6.5 13.6 %all_gather.6 = bf16[128,1024]{1,0:T(8,128)(2,1)} all-gather(bf16[128,128]{1,0:T(8,128)(2,1)} %param.13), channel_id=1, replica_groups=mesh['group'=8,'member'=32] {'group'}, dimensions={1}, use_global_device_ids=true | all-gather | bytes 294912 | tf_op jit(solution)/shard_map/all_gather | solution.py:34
  21.6 11.4 %all-to-all-start = ((s32[32,1,16]{2,1,0:T(1,128)}), s32[32,1,16]{2,1,0:T(1,128)S(1)}, u32[]{:S(2)}, u32[]{:S(2)}) async-start(s32[32,1,16]{2,1,0:T(1,128)} %concatenate.9), calls=%async_computation | async-start | bytes 32768 | tf_op jit(solution)/shard_map/all_to_all | solution.py:19
  33.0 8.6 %all-to-all-done = s32[32,1,16]{2,1,0:T(1,128)S(1)} async-done(((s32[32,1,16]{2,1,0:T(1,128)}), s32[32,1,16]{2,1,0:T(1,128)S(1)}, u32[]{:S(2)}, u32[]{:S(2)}) %all-to-all-start) | async-done | bytes 2080 | tf_op jit(solution)/shard_map/all_to_all | solution.py:19
  41.9 2.8 %gather_fusion = bf16[32,64,1024]{2,1,0:T(8,128)(2,1)} fusion(bf16[4,64,1024]{2,1,0:T(8,128)(2,1)S(1)} %copy-done, s32[1024]{0:T(1024)S(1)} %pad_clamp_fusion.1), kind=kCustom, calls=%fused_computation | custom fusion | bytes 8388736 | tf_op jit(solution)/shard_map/gather | solution.py:58
  44.7 4.5 %bitcast_select_fusion.4 = bf16[32,1,64,1024]{3,2,1,0:T(8,128)(2,1)} fusion(bf16[32,64,1024]{2,1,0:T(8,128)(2,1)} %gather_fusion, pred[32]{0:T(512)(128)(4,1)S(1)} %reduce_or.19), kind=kLoop, calls=%fused_computation.31 | loop fusion | flops 2097152 | bytes 8388640 | tf_op jit(solution)/shard_map/jit(_where)/select_n | solution.py:57
  49.2 6.1 %all-to-all-start.1 = ((bf16[32,1,64,1024]{3,2,1,0:T(8,128)(2,1)}), bf16[32,1,64,1024]{3,2,1,0:T(8,128)(2,1)}, u32[]{:S(2)}, u32[]{:S(2)}) async-start(bf16[32,1,64,1024]{3,2,1,0:T(8,128)(2,1)} %bitcast_select_fusion.4), calls=%async_computation.1 | async-start | bytes 8388608 | tf_op jit(solution)/shard_map/all_to_all | solution.py:60
  56.3 5.4 %copy.43 = bf16[32,8,64,128]{3,2,1,0:T(8,128)(2,1)} copy(bf16[32,8,64,128]{3,1,2,0:T(8,128)(2,1)} %bitcast.134) | data formatting | bytes 8388608
  62.0 1.9 fusion.30
  64.0 122.8 %all-to-all-done.1 = bf16[32,1,64,1024]{3,2,1,0:T(8,128)(2,1)} async-done(((bf16[32,1,64,1024]{3,2,1,0:T(8,128)(2,1)}), bf16[32,1,64,1024]{3,2,1,0:T(8,128)(2,1)}, u32[]{:S(2)}, u32[]{:S(2)}) %all-to-all-start.1) | async-done | bytes 4194336 | tf_op jit(solution)/shard_map/all_to_all | solution.py:60
  186.8 2.9 %gather_fusion.1 = bf16[16,64,1024]{2,1,0:T(8,128)(2,1)S(1)} fusion(bf16[32,64,1024]{2,1,0:T(8,128)(2,1)} %bitcast.7, s32[1024]{0:T(1024)S(1)} %pad_clamp_fusion), kind=kCustom, calls=%fused_computation.1 | custom fusion | bytes 4194368 | tf_op jit(solution)/shard_map/gather | solution.py:65
  189.7 6.3 %convolution_convert_fusion = bf16[256,1024]{1,0:T(8,128)(2,1)S(1)} fusion(bf16[256,4096]{1,0:T(8,128)(2,1)} %fusion.30, bf16[4096,1024]{1,0:T(8,128)(2,1)} %all-gather.2.cloned.1.call-done), kind=kOutput, calls=%fused_computation.40 | convolution fusion | flops 2147745792 | bytes 11010048 | tf_op jit(solution)/shard_map/dot_general | solution.py:35
  196.1 2.6 convert_select_fusion
  198.6 2.9 %copy.31 = bf16[2,512,1024]{1,2,0:T(8,128)(2,1)S(1)} copy(bf16[2,512,1024]{2,1,0:T(8,128)(2,1)} %bitcast.133) | data formatting | bytes 4194304 | tf_op jit(solution)/shard_map/reshape | solution.py:74
  201.5 1.7 pad_maximum_fusion
  203.2 59.2 %while.11 = (s32[]{:T(128)}, bf16[2,128,8192]{2,1,0:T(8,128)(2,1)}, bf16[2,640,4,128]{1,3,2,0:T(8,128)(2,1)}, bf16[2,640,4,128]{1,3,2,0:T(8,128)(2,1)}, bf16[2,1...) while((s32[]{:T(128)}, bf16[2,128,8192]{2,1,0:T(8,128)(2,1)}, ...), condition=%wide.region_8.9_spmd.clone, body=%wide.region_5.8_spmd.clone.sunk | while | flops 2717024768 | bytes 60265176 | solution.py:100
  203.2 2.0 constant_dynamic-slice_fusion.2
  205.5 12.5 %fusion.73 = (f32[4,16,128]{2,1,0:T(8,128)S(1)}, f32[4,16,128,640]{2,3,1,0:T(8,128)}) fusion(pred[128,640]{0,1:T(8,128)(4,1)S(1)} %fusion.72, bf16[1,128,4,16,128]{4,3,2,1,0:T(8,128)(2,1)S(1)} %constant_dynamic-slice_fusion.2, bf16[2,640,4,128]{1,3,2,0:T(8,128)(2,1)} %get-tuple-element.170, s32[]{:T(128)} %get-tuple-element.159), kind=kOutput, calls=%fused_computation.92.clone.1 | convolution fusion | flops 1363149440 | bytes 23839232 | tf_op jit(solution)/shard_map/while/body/eval_jaxpr/sub | solution.py:93
  218.0 10.4 %fusion.74 = bf16[4,128,16,128]{3,1,2,0:T(8,128)(2,1)} fusion(f32[4,16,128,640]{2,3,1,0:T(8,128)} %get-tuple-element.149, f32[4,16,128]{2,1,0:T(8,128)S(1)} %get-tuple-element.150, bf16[2,640,4,128]{1,3,2,0:T(8,128)(2,1)} %get-tuple-element.169, s32[]{:T(128)} %get-tuple-element.159), kind=kOutput, calls=%fused_computation.14.clone.1 | convolution fusion | flops 1353711616 | bytes 23757312 | tf_op jit(solution)/shard_map/while/body/eval_jaxpr/kgts,skd->tkgd/dot_general | solution.py:95
  228.5 2.9 %copy.58 = bf16[1,128,8192]{2,1,0:T(8,128)(2,1)S(1)} copy(bf16[1,128,8192]{1,2,0:T(8,128)(2,1)} %bitcast.131) | data formatting | bytes 4194304 | tf_op jit(solution)/shard_map/while/body/jit(dynamic_update_index_in_dim)/dynamic_update_slice | solution.py:100
  231.4 1.5 constant_dynamic-update-slice_fusion.2
  232.8 2.0 constant_dynamic-slice_fusion.2
  235.1 12.5 %fusion.73 = (f32[4,16,128]{2,1,0:T(8,128)S(1)}, f32[4,16,128,640]{2,3,1,0:T(8,128)}) fusion(pred[128,640]{0,1:T(8,128)(4,1)S(1)} %fusion.72, bf16[1,128,4,16,128]{4,3,2,1,0:T(8,128)(2,1)S(1)} %constant_dynamic-slice_fusion.2, bf16[2,640,4,128]{1,3,2,0:T(8,128)(2,1)} %get-tuple-element.170, s32[]{:T(128)} %get-tuple-element.159), kind=kOutput, calls=%fused_computation.92.clone.1 | convolution fusion | flops 1363149440 | bytes 23839232 | tf_op jit(solution)/shard_map/while/body/eval_jaxpr/sub | solution.py:93
  247.6 10.4 %fusion.74 = bf16[4,128,16,128]{3,1,2,0:T(8,128)(2,1)} fusion(f32[4,16,128,640]{2,3,1,0:T(8,128)} %get-tuple-element.149, f32[4,16,128]{2,1,0:T(8,128)S(1)} %get-tuple-element.150, bf16[2,640,4,128]{1,3,2,0:T(8,128)(2,1)} %get-tuple-element.169, s32[]{:T(128)} %get-tuple-element.159), kind=kOutput, calls=%fused_computation.14.clone.1 | convolution fusion | flops 1353711616 | bytes 23757312 | tf_op jit(solution)/shard_map/while/body/eval_jaxpr/kgts,skd->tkgd/dot_general | solution.py:95
  258.1 2.9 %copy.58 = bf16[1,128,8192]{2,1,0:T(8,128)(2,1)S(1)} copy(bf16[1,128,8192]{1,2,0:T(8,128)(2,1)} %bitcast.131) | data formatting | bytes 4194304 | tf_op jit(solution)/shard_map/while/body/jit(dynamic_update_index_in_dim)/dynamic_update_slice | solution.py:100
  (38 shorter events, 6.0 us)
Async XLA Ops:
  6.5 35.3 %copy-start = (bf16[4,64,1024]{2,1,0:T(8,128)(2,1)S(1)}, bf16[4,64,1024]{2,1,0:T(8,128)(2,1)}, u32[]{:S(2)}) copy-start(bf16[4,64,1024]{2,1,0:T(8,128)(2,1)} %param.11) | copy-start | bytes 1572868
  6.5 183.2 %all-gather.2.cloned.1.call-start = ((), (), s32[]{:S(2)}) async-start(), calls=%async_computation.2 | async-start | bytes 8650752 | tf_op jit(solution)/shard_map/all_gather | solution.py:37
  21.6 20.0 %all-to-all-start = ((s32[32,1,16]{2,1,0:T(1,128)}), s32[32,1,16]{2,1,0:T(1,128)S(1)}, u32[]{:S(2)}, u32[]{:S(2)}) async-start(s32[32,1,16]{2,1,0:T(1,128)} %concatenate.9), calls=%async_computation | async-start | bytes 32768 | tf_op jit(solution)/shard_map/all_to_all | solution.py:19
  49.2 6.1 %copy-start.5 = (s32[2,8]{1,0:T(2,128)S(1)}, s32[2,8]{1,0:T(2,128)}, u32[]{:S(2)}) copy-start(s32[2,8]{1,0:T(2,128)} %param.14) | copy-start | bytes 196
  49.2 6.2 %copy-start.2 = (bf16[2,8,16,4096]{3,2,1,0:T(8,128)(2,1)S(1)}, bf16[2,8,16,4096]{3,2,1,0:T(8,128)(2,1)}, u32[]{:S(2)}) copy-start(bf16[2,8,16,4096]{3,2,1,0:T(8,128)(2,1)} %param.12) | copy-start | bytes 6291460
  49.2 6.8 %copy-start.3 = (bf16[256,1024]{1,0:T(8,128)(2,1)S(1)}, bf16[256,1024]{1,0:T(8,128)(2,1)}, u32[]{:S(2)}) copy-start(bf16[256,1024]{1,0:T(8,128)(2,1)} %param.10) | copy-start | bytes 1572868
  49.2 137.6 %all-to-all-start.1 = ((bf16[32,1,64,1024]{3,2,1,0:T(8,128)(2,1)}), bf16[32,1,64,1024]{3,2,1,0:T(8,128)(2,1)}, u32[]{:S(2)}, u32[]{:S(2)}) async-start(bf16[32,1,64,1024]{3,2,1,0:T(8,128)(2,1)} %bitcast_select_fusion.4), calls=%async_computation.1 | async-start | bytes 8388608 | tf_op jit(solution)/shard_map/all_to_all | solution.py:60
  56.3 5.6 %copy-start.4 = (s32[2,8,16]{2,1,0:T(8,128)S(1)}, s32[2,8,16]{2,1,0:T(8,128)}, u32[]{:S(2)}) copy-start(s32[2,8,16]{2,1,0:T(8,128)} %param.15) | copy-start | bytes 3076
  262.4 1.0 copy-start.1
Sparse Core Ops, SparseCore 0:
  20.3 167.9 all-gather.1
